TPU v7x, 512 devices: a whole 4x8x8 slice. The times are simulated.
512 devices in a mesh: expert: 32 (over y_lo, z, core), dp: 16 (over y_hi, x).
Axes of the slice: x: 4, y: 8 (y_hi: 4, y_lo: 2; y = y_hi * 2 + y_lo), z: 8, core: 2. Of those that a mesh axis runs over, the one named last changes fastest.
Arguments:
- tokens: bfloat16 [65536, 3584], P(('expert', 'dp')), may hold values from -6 to 6
- expert_ids: int32 [65536, 8], P(('expert', 'dp')), may hold values from 0 to 255, all different within a row
- gate_probs: float32 [65536, 8], P(('expert', 'dp')), may hold values from 0.02 to 0.5
- out_grad: bfloat16 [65536, 3584], P(('expert', 'dp')), may hold values from -6 to 6
- w_gate: bfloat16 [32, 1024, 3584], P('expert', 'dp'), may hold values from -0.09375 to 0.09375
- w_up: bfloat16 [32, 1024, 3584], P('expert', 'dp'), may hold values from -0.09375 to 0.09375
- w_down: bfloat16 [32, 1024, 3584], P('expert', 'dp'), may hold values from -0.1875 to 0.1875
Outputs:
- grad_gate: bfloat16 [32, 1024, 3584], P('expert', 'dp')
- grad_up: bfloat16 [32, 1024, 3584], P('expert', 'dp')
- grad_down: bfloat16 [32, 1024, 3584], P('expert', 'dp')
All inputs are finite; a program needn't handle non-finite values.
Results may differ from a plain program's by a relative error of at most 0.0058.
Values may be sent and summed in bfloat16 or wider, within the bound.
A program may use at most 64 MiB of HBM per device.

v0:
```python
import jax
import jax.numpy as jnp
from jax import lax
from jax.sharding import PartitionSpec as P

CAP = 2


def local_factors(rows_x, rows_dy, weight_gate, weight_up, weight_down):
    contract = (((1,), (1,)), ((), ()))
    gate_pre = lax.dot_general(rows_x, weight_gate, contract, preferred_element_type=jnp.float32)
    up_pre = lax.dot_general(rows_x, weight_up, contract, preferred_element_type=jnp.float32)
    back_grad = lax.dot_general(rows_dy, weight_down, contract, preferred_element_type=jnp.float32)
    sig_gate = jax.nn.sigmoid(gate_pre)
    act_gate = gate_pre * sig_gate
    hidden = (act_gate * up_pre).astype(jnp.bfloat16)
    d_gate = (back_grad * up_pre * sig_gate * (1.0 + gate_pre * (1.0 - sig_gate))).astype(
        jnp.bfloat16
    )
    d_up = (back_grad * act_gate).astype(jnp.bfloat16)
    return (d_gate, d_up, hidden)


def outer_sum(factor, rows):
    return lax.dot_general(
        factor, rows, (((0,), (0,)), ((), ())), preferred_element_type=jnp.float32
    )


def local(tokens, expert_ids, gate_probs, out_grad, w_gate, w_up, w_down):
    n_expert = lax.axis_size("expert")
    experts_all = w_gate.shape[0] * n_expert
    tok_rows, top_count = expert_ids.shape
    feature_count = tokens.shape[1]
    flat_ids = expert_ids.reshape(-1)
    expert_range = jnp.arange(experts_all, dtype=jnp.int32)
    onehot = (flat_ids[:, None] == expert_range[None, :]).astype(jnp.int32)
    before = jnp.cumsum(onehot, axis=0) - onehot
    slot_rank = jnp.sum(before * onehot, axis=1)
    kept_mask = (flat_ids < experts_all) & (slot_rank < CAP)
    slot_index = jnp.where(kept_mask, flat_ids * CAP + slot_rank, -1)
    slot_range = jnp.arange(experts_all * CAP, dtype=jnp.int32)
    matches = (slot_index[None, :] == slot_range[:, None]).astype(jnp.float32)
    matches = matches.reshape(experts_all * CAP, tok_rows, top_count)
    picker = jnp.sum(matches, axis=2).astype(jnp.bfloat16)
    slot_prob = jnp.sum(matches * gate_probs[None, :, :], axis=(1, 2))
    sent_x = jnp.dot(picker, tokens, preferred_element_type=jnp.float32).astype(jnp.bfloat16)
    sent_dy = (
        jnp.dot(picker, out_grad, preferred_element_type=jnp.float32) * slot_prob[:, None]
    ).astype(jnp.bfloat16)
    sent_x = sent_x.reshape(experts_all, CAP, feature_count)
    sent_dy = sent_dy.reshape(experts_all, CAP, feature_count)
    recv_x, recv_dy = (
        lax.all_to_all(sent_x, "expert", split_axis=0, concat_axis=0, tiled=True),
        lax.all_to_all(sent_dy, "expert", split_axis=0, concat_axis=0, tiled=True),
    )
    rows_x = recv_x.reshape(-1, feature_count)
    rows_dy = recv_dy.reshape(-1, feature_count)
    piece_x = lax.all_gather(rows_x, "dp", axis=0, tiled=True)
    piece_dy = lax.all_gather(rows_dy, "dp", axis=0, tiled=True)
    d_gate, d_up, hidden = local_factors(piece_x, piece_dy, w_gate[0], w_up[0], w_down[0])
    term_gate = outer_sum(d_gate, piece_x)
    term_up = outer_sum(d_up, piece_x)
    term_down = outer_sum(hidden, piece_dy)
    return (
        term_gate.astype(jnp.bfloat16)[None],
        term_up.astype(jnp.bfloat16)[None],
        term_down.astype(jnp.bfloat16)[None],
    )


def solution(mesh):
    in_specs = (
        P(("expert", "dp"), None),
        P(("expert", "dp"), None),
        P(("expert", "dp"), None),
        P(("expert", "dp"), None),
        P("expert", "dp", None),
        P("expert", "dp", None),
        P("expert", "dp", None),
    )
    out_specs = (P("expert", "dp", None), P("expert", "dp", None), P("expert", "dp", None))
    return jax.shard_map(local, mesh=mesh, in_specs=in_specs, out_specs=out_specs, check_vma=False)
```

profile of v0, /device:TPU:1, one launch (start us, length us, event | category | flops | bytes accessed | tf_op | source)
XLA Modules:
  0.0 293.1 jit_solution(2632505541616493926)
XLA Ops:
  7.2 0.0 copy-start
  7.2 0.0 copy-start.3
  7.2 0.0 all-gather.5.cloned.1.call-start
  7.2 0.9 copy.30
  8.1 0.1 eq.43
  8.2 0.1 eq.39
  8.3 9.0 %reduce-window.6 = s32[32,8,128]{2,1,0:T(8,128)S(1)} reduce-window(s32[32,8,128]{2,1,0:T(8,128)S(1)} %fusion.15, s32[]{:T(128)} %constant.4.clone.1), window={size=1x1x128 pad=0_0x0_0x127_0}, to_apply=%region_0.0 | reduce-window | flops 4161536 | bytes 262148 | tf_op jit(solution)/shard_map/reduce-window
  17.3 0.1 slice.8
  17.4 0.1 copy.32
  17.6 0.1 copy.33
  17.7 0.1 broadcast_add_fusion
  17.8 0.1 reduce_sum.30
  18.0 0.7 add_select_fusion
  18.7 1.2 select_reduce_fusion
  19.9 0.0 copy-done
  19.9 0.3 convolution_convert_fusion.3
  20.2 0.2 reshape.64
  20.4 27.1 %all_to_all.10 = bf16[32,2,3584]{2,1,0:T(2,128)(2,1)S(1)} all-to-all(bf16[32,2,3584]{2,1,0:T(2,128)(2,1)S(1)} %reshape.64), channel_id=1, replica_groups=mesh['expert'=32,'dp'=16] {'expert'}, dimensions={0} | all-to-all | bytes 917504 | tf_op jit(solution)/shard_map/all_to_all | solution.py:54
  47.5 0.0 copy-start.4
  47.5 0.9 reshape.65
  48.4 0.0 all-gather.5.cloned.1.call-update
  48.4 0.0 all-gather.3.cloned.1.call-start
  48.5 1.5 fusion
  49.9 0.2 reshape.62
  50.1 19.5 %all_to_all.11 = bf16[32,2,3584]{2,1,0:T(2,128)(2,1)S(1)} all-to-all(bf16[32,2,3584]{2,1,0:T(2,128)(2,1)S(1)} %reshape.62), channel_id=1, replica_groups=mesh['expert'=32,'dp'=16] {'expert'}, dimensions={0} | all-to-all | bytes 917504 | tf_op jit(solution)/shard_map/all_to_all | solution.py:55
  69.6 0.9 reshape.63
  70.6 0.0 all-gather.3.cloned.1.call-update
  70.6 0.0 copy-start.5
  70.6 85.9 %all-gather.5.cloned.1.call-done = bf16[1024,3584]{1,0:T(8,128)(2,1)} async-done(((bf16[64,3584]{1,0:T(8,128)(2,1)}), bf16[1024,3584]{1,0:T(8,128)(2,1)}) %all-gather.5.cloned.1.call-update) | async-done | bytes 7340048 | tf_op jit(solution)/shard_map/all_gather | solution.py:59
  156.5 0.0 copy-done.3
  156.5 0.0 copy-start.1
  156.5 5.5 %fusion.4 = f32[1024,64]{0,1:T(8,128)S(1)} fusion(bf16[1024,3584]{1,0:T(8,128)(2,1)} %all-gather.5.cloned.1.call-done, bf16[1,64,3584]{2,1,0:T(8,128)(2,1)S(1)} %copy-done.3), kind=kOutput, calls=%fused_computation.9 | convolution fusion | flops 469762048 | bytes 8060928 | tf_op jit(solution)/shard_map/dot_general | solution.py:11
  162.1 0.0 copy-done.4
  162.1 0.0 copy-done.1
  162.1 2.3 fusion.6
  164.4 106.6 %all-gather.3.cloned.1.call-done = bf16[1024,3584]{1,0:T(8,128)(2,1)} async-done(((bf16[64,3584]{1,0:T(8,128)(2,1)}), bf16[1024,3584]{1,0:T(8,128)(2,1)}) %all-gather.3.cloned.1.call-update) | async-done | bytes 7340048 | tf_op jit(solution)/shard_map/all_gather | solution.py:60
  271.0 0.0 copy-done.5
  271.0 0.0 copy-start.2
  271.0 5.5 %fusion.8 = f32[1024,64]{0,1:T(8,128)S(1)} fusion(bf16[1024,3584]{1,0:T(8,128)(2,1)} %all-gather.3.cloned.1.call-done, bf16[1,64,3584]{2,1,0:T(8,128)(2,1)S(1)} %copy-done.5), kind=kOutput, calls=%fused_computation.13 | convolution fusion | flops 469762048 | bytes 8060928 | tf_op jit(solution)/shard_map/dot_general | solution.py:13
  276.6 0.0 copy-done.2
  276.6 0.0 slice-start
  276.6 2.1 fusion.3
  278.7 0.0 slice-start.1
  278.7 5.4 %fusion.1 = bf16[1,64,3584]{2,1,0:T(8,128)(2,1)} fusion(bf16[1024,3584]{1,0:T(8,128)(2,1)} %all-gather.5.cloned.1.call-done, f32[1024,64]{0,1:T(8,128)S(1)} %fusion.4, f32[1024,64]{0,1:T(8,128)S(1)} %fusion.8, f32[1024,64]{0,1:T(8,128)S(1)} %fusion.6), kind=kOutput, calls=%fused_computation.6 | convolution fusion | flops 470646784 | bytes 8585216 | tf_op jit(solution)/shard_map/dot_general | solution.py:25
  284.1 0.0 slice-done
  284.1 0.0 slice-done.1
  284.1 2.1 fusion.2
  (6 shorter events, 0.1 us)
Async XLA Ops:
  7.2 12.8 %copy-start = (bf16[128,3584]{1,0:T(8,128)(2,1)S(1)}, bf16[128,3584]{1,0:T(8,128)(2,1)}, u32[]{:S(2)}) copy-start(bf16[128,3584]{1,0:T(8,128)(2,1)} %param.7) | copy-start | bytes 2752516
  7.2 149.3 %copy-start.3 = (bf16[1,64,3584]{2,1,0:T(8,128)(2,1)S(1)}, bf16[1,64,3584]{2,1,0:T(8,128)(2,1)}, u32[]{:S(2)}) copy-start(bf16[1,64,3584]{2,1,0:T(8,128)(2,1)} %param.11) | copy-start | bytes 1376260
  7.2 149.3 %all-gather.5.cloned.1.call-start = ((), (), s32[]{:S(2)}) async-start(), calls=%async_computation.3 | async-start | bytes 7798784 | tf_op jit(solution)/shard_map/all_gather | solution.py:59
  47.5 114.6 %copy-start.4 = (bf16[1,64,3584]{2,1,0:T(8,128)(2,1)S(1)}, bf16[1,64,3584]{2,1,0:T(8,128)(2,1)}, u32[]{:S(2)}) copy-start(bf16[1,64,3584]{2,1,0:T(8,128)(2,1)} %param.12) | copy-start | bytes 1376260
  48.4 222.6 %all-gather.3.cloned.1.call-start = ((), (), s32[]{:S(2)}) async-start(), calls=%async_computation.2 | async-start | bytes 7798784 | tf_op jit(solution)/shard_map/all_gather | solution.py:60
  70.6 200.4 %copy-start.5 = (bf16[1,64,3584]{2,1,0:T(8,128)(2,1)S(1)}, bf16[1,64,3584]{2,1,0:T(8,128)(2,1)}, u32[]{:S(2)}) copy-start(bf16[1,64,3584]{2,1,0:T(8,128)(2,1)} %param.13) | copy-start | bytes 1376260
  156.5 5.6 %copy-start.1 = (bf16[1024,3584]{1,0:T(8,128)(2,1)S(1)}, bf16[1024,3584]{1,0:T(8,128)(2,1)}, u32[]{:S(2)}) copy-start(bf16[1024,3584]{1,0:T(8,128)(2,1)} %all-gather.5.cloned.1.call-done) | copy-start | bytes 22020100
  271.0 5.5 %copy-start.2 = (bf16[1024,3584]{1,0:T(8,128)(2,1)S(1)}, bf16[1024,3584]{1,0:T(8,128)(2,1)}, u32[]{:S(2)}) copy-start(bf16[1024,3584]{1,0:T(8,128)(2,1)} %all-gather.3.cloned.1.call-done) | copy-start | bytes 22020100
  276.6 7.5 %slice-start = ((s8[7340032]{0:T(1024)(128)(4,1)}), s8[4194304]{0:T(1024)(128)(4,1)S(1)}, s32[]{:S(2)}) async-start(s8[7340032]{0:T(1024)(128)(4,1)} %bitcast.43), calls=%async_computation.4 | async-start | bytes 8388608
  278.7 5.4 %slice-start.1 = ((s8[7340032]{0:T(1024)(128)(4,1)}), s8[3145728]{0:T(1024)(128)(4,1)S(1)}, s32[]{:S(2)}) async-start(s8[7340032]{0:T(1024)(128)(4,1)} %bitcast.43), calls=%async_computation.5 | async-start | bytes 6291456
Sparse Core Ops, SparseCore 0:
  48.6 107.9 all-gather.4
  160.1 110.8 all-gather.2
where the time goes:
time: 293 us
  waiting for transfers between devices  193 us (66%)
  blocking collectives  46.6 us (16%)
  matrix products  24.7 us (8%)
  between operations  14.2 us (5%)
  other arithmetic  11.2 us (4%)
  local copies, waits for them, and re-layouts  3.76 us (1%)
    all_gather x1, waiting for transfers between devices, local(): piece_dy = lax.all_gather(rows_dy, 'dp', axis=0, tiled=True)  107 us
    all_gather x1, waiting for transfers between devices, local(): piece_x = lax.all_gather(rows_x, 'dp', axis=0, tiled=True)  85.9 us
    all_to_all x1, blocking collectives, local(): lax.all_to_all(sent_x, 'expert', split_axis=0, concat_axis=0, tiled=True)  27.1 us
    all_to_all x1, blocking collectives, local(): lax.all_to_all(sent_dy, 'expert', split_axis=0, concat_axis=0, tiled=True)  19.5 us
    dot_general x3, matrix products, outer_sum(): lax.dot_general(factor, rows, (((0,), (0,)), ((), ())), preferred_element...  9.65 us
    another operation x3, other arithmetic  9.15 us
  transfers between devices with their start and end apart: 2, of which 2 were waited for; matrix products, arithmetic and copies ran while one was open for 4% of the time, Pallas kernels for 0%

commit v1 on v0

v1 whole, which is shorter than its diff:
```python
import functools

import jax
import jax.numpy as jnp
from jax import lax
from jax.experimental import pallas as pl
from jax.experimental.pallas import tpu as pltpu
from jax.sharding import PartitionSpec as P

CAP = 2
NX = 4
NH = 4
MESH = pl.DeviceIdType.MESH
NT = (((1,), (1,)), ((), ()))
BF16 = jnp.bfloat16
F32 = jnp.float32


def kernel(
    sx, sdy, wg, wu, wd, og, ou, od,
    recv, blk, xq, wq, psend, precv, pown, fac, acc, gbuf,
    disp_s, disp_r, disp_l, w_s, w_r, w_l, xa_s, xa_r, xa_l,
    y_s, y_r, rs_s, rs_r, ag_s, ag_r, o_s, o_r, o_l,
):
    n_exp = recv.shape[1]
    ff = wg.shape[0]
    quarter = xq.shape[-1]
    rows = blk.shape[1]
    me = lax.axis_index("expert")
    dp = lax.axis_index("dp")
    h = dp // NX
    x = dp % NX
    left_h = (h + NH - 1) % NH
    right_h = (h + 1) % NH
    far_h = (h + 2) % NH

    def peer_e(k):
        return lax.rem(me + k, n_exp)

    def peer_x(k):
        return (x + k) % NX

    def dp_x(k):
        return h * NX + peer_x(k)

    def cols(k):
        return pl.ds(pl.multiple_of(k * quarter, 128), quarter)

    def drain(ref, sem):
        pltpu.make_async_copy(ref, ref, sem).wait()

    barrier = pltpu.get_barrier_semaphore()

    def greet(k, carry):
        pl.semaphore_signal(barrier, inc=1, device_id={"expert": peer_e(k)}, device_id_type=MESH)
        return carry

    lax.fori_loop(1, n_exp, greet, 0)
    for k in (1, 3, 2):
        pl.semaphore_signal(barrier, inc=1, device_id={"dp": dp_x(k)}, device_id_type=MESH)
    for hh in (left_h, right_h):
        pl.semaphore_signal(barrier, inc=1, device_id={"dp": hh * NX + x}, device_id_type=MESH)
    pl.semaphore_wait(barrier, n_exp - 1 + 3 + 2)

    sent = (sx, sdy)

    def dispatch(kind):
        def send(k, carry):
            e = peer_e(k)
            pltpu.make_async_remote_copy(
                src_ref=sent[kind].at[e], dst_ref=recv.at[kind, me],
                send_sem=disp_s.at[kind], recv_sem=disp_r.at[kind],
                device_id={"expert": e}, device_id_type=MESH,
            ).start()
            return carry

        lax.fori_loop(1, n_exp, send, 0)
        pltpu.make_async_copy(sent[kind].at[me], recv.at[kind, me], disp_l.at[kind]).start()

    dispatch(0)
    weights = (wg, wu, wd)
    for k in (2, 1, 3):
        for i in range(3):
            pltpu.make_async_remote_copy(
                src_ref=weights[i].at[:, cols(peer_x(k))], dst_ref=wq.at[i, x],
                send_sem=w_s, recv_sem=w_r,
                device_id={"dp": dp_x(k)}, device_id_type=MESH,
            ).start()
    for i in range(3):
        pltpu.make_async_copy(weights[i].at[:, cols(x)], wq.at[i, x], w_l.at[i]).start()
    dispatch(1)

    def y_copy(kind, way, turn, hh, j0):
        to = right_h if way == 0 else left_h
        return pltpu.make_async_remote_copy(
            src_ref=xq.at[kind, hh, pl.ds(j0, 2)], dst_ref=xq.at[kind, hh, pl.ds(j0, 2)],
            send_sem=y_s.at[kind, way, turn], recv_sem=y_r.at[kind, way, turn],
            device_id={"dp": to * NX + x}, device_id_type=MESH,
        )

    for kind in range(2):
        drain(recv.at[kind, pl.ds(0, n_exp - 1)], disp_r.at[kind])
        pltpu.make_async_copy(sent[kind].at[me], recv.at[kind, me], disp_l.at[kind]).wait()
        for g in range(rows // 16):
            blk[kind, 16 * g:16 * (g + 1), :] = jnp.concatenate(
                [recv[kind, 8 * g + i] for i in range(8)], axis=0
            )
        for k in (2, 1, 3):
            pltpu.make_async_remote_copy(
                src_ref=blk.at[kind, :, cols(peer_x(k))], dst_ref=xq.at[kind, h, x],
                send_sem=xa_s.at[kind], recv_sem=xa_r.at[kind],
                device_id={"dp": dp_x(k)}, device_id_type=MESH,
            ).start()
        mine = pltpu.make_async_copy(blk.at[kind, :, cols(x)], xq.at[kind, h, x], xa_l.at[kind])
        mine.start()
        mine.wait()
        drain(xq.at[kind, h, pl.ds(0, 3)], xa_r.at[kind])
        y_copy(kind, 0, 0, h, 0).start()
        y_copy(kind, 1, 0, h, 2).start()
        y_copy(kind, 0, 1, h, 2).start()
        y_copy(kind, 1, 1, h, 0).start()

    drain(wq.at[:, pl.ds(0, 3)], w_r)
    for i in range(3):
        pltpu.make_async_copy(weights[i].at[:, cols(x)], wq.at[i, x], w_l.at[i]).wait()

    def chunk(kind, hh):
        return xq[kind, hh].reshape(NX * rows, quarter)

    def partial_sums(o, hh):
        both = wq[0:2].reshape(2 * NX * ff, quarter)
        down = wq[2].reshape(NX * ff, quarter)
        pre = lax.dot_general(both, chunk(0, hh), NT, preferred_element_type=F32)
        back = lax.dot_general(down, chunk(1, hh), NT, preferred_element_type=F32)
        parts = (pre[: NX * ff], pre[NX * ff :], back)
        for i in range(3):
            piece = parts[i].reshape(NX, ff, NX * rows)
            pown[o, i] = piece
            psend[o, :, i] = piece.astype(BF16)
        for k in (2, 1, 3):
            pltpu.make_async_remote_copy(
                src_ref=psend.at[o, peer_x(k)], dst_ref=precv.at[o, k - 1],
                send_sem=rs_s.at[o], recv_sem=rs_r.at[o],
                device_id={"dp": dp_x(k)}, device_id_type=MESH,
            ).start()

    def factors(o):
        drain(precv.at[o], rs_r.at[o])
        total = []
        for i in range(3):
            v = pown[o, i, x]
            for k in range(3):
                v = v + precv[o, k, i].astype(F32)
            total.append(v)
        gate_pre, up_pre, back_grad = total
        sig = jax.nn.sigmoid(gate_pre)
        act = gate_pre * sig
        fac[o, 0, x] = (back_grad * up_pre * sig * (1.0 + gate_pre * (1.0 - sig))).astype(BF16)
        fac[o, 1, x] = (back_grad * act).astype(BF16)
        fac[o, 2, x] = (act * up_pre).astype(BF16)
        for k in (2, 1, 3):
            pltpu.make_async_remote_copy(
                src_ref=fac.at[o, :, x], dst_ref=fac.at[o, :, x],
                send_sem=ag_s.at[o], recv_sem=ag_r.at[o],
                device_id={"dp": dp_x(k)}, device_id_type=MESH,
            ).start()

    outs = (og, ou, od)

    def products(o, hh):
        drain(fac.at[o, :, pl.ds(0, 3)], ag_r.at[o])
        for i in range(3):
            left = fac[o, i].reshape(NX * ff, NX * rows)
            term = jnp.dot(left, chunk(1 if i == 2 else 0, hh), preferred_element_type=F32)
            if o == 0:
                acc[i] = term
            elif o < 3:
                acc[i] += term
            else:
                gbuf[i] = (acc[i] + term).astype(BF16).reshape(NX, ff, quarter)
                for k in (2, 1, 3):
                    pltpu.make_async_remote_copy(
                        src_ref=gbuf.at[i, peer_x(k)], dst_ref=outs[i].at[:, cols(x)],
                        send_sem=o_s.at[i], recv_sem=o_r.at[i],
                        device_id={"dp": dp_x(k)}, device_id_type=MESH,
                    ).start()
                pltpu.make_async_copy(gbuf.at[i, x], outs[i].at[:, cols(x)], o_l.at[i]).start()

    def arrived(kind, way, turn):
        y_copy(kind, way, turn, h, 0).wait_recv()

    partial_sums(0, h)
    for kind in range(2):
        arrived(kind, 0, 0)
        y_copy(kind, 0, 2, left_h, 0).start()
        arrived(kind, 1, 0)
        y_copy(kind, 1, 2, right_h, 2).start()
        if kind == 0:
            factors(0)
        arrived(kind, 0, 1)
        arrived(kind, 1, 1)
    partial_sums(1, left_h)
    partial_sums(2, right_h)
    products(0, h)
    factors(1)
    factors(2)
    products(1, left_h)
    products(2, right_h)
    for kind in range(2):
        arrived(kind, 0, 2)
        arrived(kind, 1, 2)
    partial_sums(3, far_h)
    factors(3)
    products(3, far_h)

    for kind in range(2):
        drain(recv.at[kind, pl.ds(0, n_exp - 1)], disp_s.at[kind])
        drain(xq.at[kind, h, pl.ds(0, 3)], xa_s.at[kind])
        for way in range(2):
            for turn in range(3):
                y_copy(kind, way, turn, h, 0).wait_send()
    drain(wq.at[:, pl.ds(0, 3)], w_s)
    for o in range(4):
        drain(precv.at[o], rs_s.at[o])
        drain(fac.at[o, :, pl.ds(0, 3)], ag_s.at[o])
    for i in range(3):
        drain(gbuf.at[i, pl.ds(0, 3)], o_r.at[i])
        drain(gbuf.at[i, pl.ds(0, 3)], o_s.at[i])
        pltpu.make_async_copy(gbuf.at[i, x], outs[i].at[:, cols(x)], o_l.at[i]).wait()


def local(tokens, expert_ids, gate_probs, out_grad, w_gate, w_up, w_down):
    n_exp = w_gate.shape[0] * lax.axis_size("expert")
    tok_rows = expert_ids.shape[0]
    d = tokens.shape[1]
    ff = w_gate.shape[1]
    quarter = d // NX
    rows = n_exp * CAP
    expert_range = jnp.arange(n_exp, dtype=jnp.int32)
    hit = expert_ids[None, :, :] == expert_range[:, None, None]
    member = jnp.sum(hit.astype(F32), axis=2)
    prob = jnp.sum(jnp.where(hit, gate_probs[None, :, :], 0.0), axis=2)
    t = jnp.arange(tok_rows, dtype=jnp.int32)
    earlier = (t[:, None] < t[None, :]).astype(BF16)
    rank = jnp.dot(member.astype(BF16), earlier, preferred_element_type=F32)
    slot = jnp.arange(CAP, dtype=jnp.int32).astype(F32)
    pick = member[:, None, :] * (rank[:, None, :] == slot[None, :, None]).astype(F32)
    slot_prob = jnp.sum(pick * prob[:, None, :], axis=2).reshape(rows)
    picker = pick.reshape(rows, tok_rows).astype(BF16)
    sent_x = jnp.dot(picker, tokens, preferred_element_type=F32).astype(BF16)
    sent_dy = (
        jnp.dot(picker, out_grad, preferred_element_type=F32) * slot_prob[:, None]
    ).astype(BF16)
    sent_x = sent_x.reshape(n_exp, CAP, d)
    sent_dy = sent_dy.reshape(n_exp, CAP, d)
    dma = pltpu.SemaphoreType.DMA
    grads = pl.pallas_call(
        kernel,
        out_shape=[jax.ShapeDtypeStruct((ff, d), BF16)] * 3,
        in_specs=[pl.BlockSpec(memory_space=pl.ANY)] * 5,
        out_specs=[pl.BlockSpec(memory_space=pl.ANY)] * 3,
        scratch_shapes=[
            pltpu.VMEM((2, n_exp, CAP, d), BF16),
            pltpu.VMEM((2, rows, d), BF16),
            pltpu.VMEM((2, NH, NX, rows, quarter), BF16),
            pltpu.VMEM((3, NX, ff, quarter), BF16),
            pltpu.VMEM((4, NX, 3, ff, NX * rows), BF16),
            pltpu.VMEM((4, 3, 3, ff, NX * rows), BF16),
            pltpu.VMEM((4, 3, NX, ff, NX * rows), F32),
            pltpu.VMEM((4, 3, NX, ff, NX * rows), BF16),
            pltpu.VMEM((3, NX * ff, quarter), F32),
            pltpu.VMEM((3, NX, ff, quarter), BF16),
            dma((2,)), dma((2,)), dma((2,)),
            dma(()), dma(()), dma((3,)),
            dma((2,)), dma((2,)), dma((2,)),
            dma((2, 2, 3)), dma((2, 2, 3)),
            dma((4,)), dma((4,)), dma((4,)), dma((4,)),
            dma((3,)), dma((3,)), dma((3,)),
        ],
        compiler_params=pltpu.CompilerParams(
            collective_id=0, has_side_effects=True, vmem_limit_bytes=56 * 1024 * 1024
        ),
    )(sent_x, sent_dy, w_gate[0], w_up[0], w_down[0])
    return tuple(g[None] for g in grads)


def solution(mesh):
    in_specs = (
        P(("expert", "dp"), None),
        P(("expert", "dp"), None),
        P(("expert", "dp"), None),
        P(("expert", "dp"), None),
        P("expert", "dp", None),
        P("expert", "dp", None),
        P("expert", "dp", None),
    )
    out_specs = (P("expert", "dp", None), P("expert", "dp", None), P("expert", "dp", None))
    return jax.shard_map(local, mesh=mesh, in_specs=in_specs, out_specs=out_specs, check_vma=False)
```

time: 293 us -> 154 us (0.53)
  the two profiles are of different devices: /device:TPU:1 before, /device:TPU:10 now
where the time goes in v1:
time: 154 us; the launch traced here: 153 us
  Pallas kernels  145 us (94%)
  local copies, waits for them, and re-layouts  6.62 us (4%)
    pallas_call x1, Pallas kernels, local(): pl.pallas_call(kernel, out_shape=[jax.ShapeDtypeStruct((ff, d), BF16)] *...  145 us
    unnamed x15, local copies, waits for them, and re-layouts  4.5 us

profile of v1, /device:TPU:10, one launch (start us, length us, event | category | flops | bytes accessed | tf_op | source)
XLA Modules:
  0.0 153.3 jit_solution(7925018088589939625)
XLA Ops:
  0.6 0.0 copy-start
  0.7 0.0 copy-start.4
  0.7 0.0 copy-start.5
  0.7 0.1 eq.43
  0.8 0.6 copy-done.4
  1.4 0.0 copy-done.5
  1.4 0.1 select_reduce_fusion
  1.5 0.1 fusion.1
  1.7 0.2 fusion.3
  1.9 0.1 mul.36
  2.0 0.1 select_convert_fusion
  2.1 0.0 copy-done
  2.1 0.0 copy-start.1
  2.1 0.3 fusion
  2.4 0.9 reshape.27.sdy
  3.3 0.0 copy-done.1
  3.3 0.3 convolution_convert_fusion
  3.6 0.9 reshape.26.sx
  4.5 144.9 %shard_map.94 = (bf16[64,3584]{1,0:T(8,128)(2,1)}, bf16[64,3584]{1,0:T(8,128)(2,1)}, bf16[64,3584]{1,0:T(8,128)(2,1)}) custom-call(bf16[32,2,3584]{2,1,0:T(2,128)(2,1)} %reshape.26.sx, bf16[32,2,3584]{2,1,0:T(2,128)(2,1)} %reshape.27.sdy, bf16[64,3584]{1,0:T(8,128)(2,1)} %bitcast.15, bf16[64,3584]{1,0:T(8,128)(2,1)} %bitcast.16, bf16[64,3584]{1,0:T(8,128)(2,1)} %bitcast.17), custom_call_target="tpu_custom_call" | custom-call | tf_op jit(solution)/shard_map/pallas_call | solution.py:257
  149.5 0.0 copy-start.3
  149.5 1.9 %copy.21 = bf16[1,64,3584]{2,1,0:T(8,128)(2,1)} copy(bf16[1,64,3584]{2,1,0:T(8,128)(2,1)} %bitcast.14) | data formatting | bytes 917504
  151.4 0.0 copy-done.3
  151.4 0.0 copy-start.2
  151.4 0.8 copy.22
  152.1 0.4 copy-done.2
  152.6 0.8 copy.23
  (4 shorter events, 0.0 us)
Async XLA Ops:
  0.6 1.5 copy-start
  0.7 0.8 copy-start.4
  0.7 0.8 copy-start.5
  2.1 1.2 copy-start.1
  149.5 1.9 %copy-start.3 = (bf16[64,3584]{1,0:T(8,128)(2,1)S(1)}, bf16[64,3584]{1,0:T(8,128)(2,1)}, u32[]{:S(2)}) copy-start(bf16[64,3584]{1,0:T(8,128)(2,1)} %get-tuple-element.7) | copy-start | bytes 1376260
  151.4 1.2 copy-start.2

commit v2 on v1

v2 whole, which is shorter than its diff:
```python
import functools

import jax
import jax.numpy as jnp
from jax import lax
from jax.experimental import pallas as pl
from jax.experimental.pallas import tpu as pltpu
from jax.sharding import PartitionSpec as P

CAP = 2
NX = 4
NH = 4
MESH = pl.DeviceIdType.MESH
NT = (((1,), (1,)), ((), ()))
BF16 = jnp.bfloat16
F32 = jnp.float32
WIDE = (0, 2)
WIDTHS = (4, 8, 4, 8, 4, 4)


def kernel(
    sx, sdy, wg, wu, wd, og, ou, od,
    recv, xq, wq, pown, psend, precv, fac, acc, gbuf,
    disp_s, disp_r, disp_l, w_s, w_r, w_l,
    y_s, y_r, rs_s, rs_r, ag_s, ag_r, o_s, o_r, o_l,
):
    n_exp = sx.shape[0]
    ff = wg.shape[0]
    quarter = xq.shape[-1]
    rows = xq.shape[-2]
    n_peer = NX * n_exp
    me = lax.axis_index("expert")
    dp = lax.axis_index("dp")
    h = dp // NX
    x = dp % NX
    left = (h + NH - 1) % NH
    right = (h + 1) % NH
    far = (h + 2) % NH
    chunks = (
        ((h, 0),),
        ((left, 0), (right, 0)),
        ((h, 1),),
        ((left, 1), (right, 1)),
        ((far, 0),),
        ((far, 1),),
    )

    def peer_x(k):
        return (x + k) % NX

    def dp_x(k):
        return h * NX + peer_x(k)

    def experts(act, odd, itself):
        half = n_exp // 2
        if not odd:
            act(lax.rem(me + half, n_exp))

        def pair(i, carry):
            act(lax.rem(me + half - (2 - odd) - 2 * i, n_exp))
            act(lax.rem(me + half + (2 - odd) + 2 * i, n_exp))
            return carry

        lax.fori_loop(0, half // 2 - (1 - odd), pair, 0)
        if itself and not odd:
            act(me)

    def cols(k):
        return pl.ds(pl.multiple_of(k * quarter, 128), quarter)

    def drain(ref, sem):
        pltpu.make_async_copy(ref, ref, sem).wait()

    barrier = pltpu.get_barrier_semaphore()

    for k in range(NX):
        def greet(e, k=k):
            pl.semaphore_signal(
                barrier, inc=1, device_id={"expert": e, "dp": dp_x(k)}, device_id_type=MESH
            )

        for odd in range(2):
            experts(greet, odd, k > 0)
    for hh in (left, right):
        pl.semaphore_signal(barrier, inc=1, device_id={"dp": hh * NX + x}, device_id_type=MESH)
    pl.semaphore_wait(barrier, n_peer - 1 + 2)

    sent = (sx, sdy)

    def slab(odd, kind):
        return recv.at[odd, (x * 2 + kind) * (n_exp // 2) + me // 2]

    def keep(kind):
        return pltpu.make_async_copy(sent[kind].at[me, :, cols(x)], slab(0, kind), disp_l.at[kind])

    def dispatch(odd):
        for k in (0, 3, 1, 2):
            for kind in range(2):
                if k == 0 and not odd:
                    keep(kind).start()

                def send(e, k=k, kind=kind):
                    pltpu.make_async_remote_copy(
                        src_ref=sent[kind].at[e, :, cols(peer_x(k))], dst_ref=slab(odd, kind),
                        send_sem=disp_s.at[odd], recv_sem=disp_r.at[odd, x],
                        device_id={"expert": e, "dp": dp_x(k)}, device_id_type=MESH,
                    ).start()

                experts(send, odd, k > 0)

    def drain_sent(odd):
        drain(recv.at[odd, pl.ds(0, n_peer - 2 + 2 * odd)], disp_s.at[odd])

    weights = (wg, wu, wd)
    dispatch(0)
    def exchange_weights():
        for i in range(3):
            for k in (2, 1, 3):
                pltpu.make_async_remote_copy(
                    src_ref=weights[i].at[:, cols(peer_x(k))], dst_ref=wq.at[i, x],
                    send_sem=w_s, recv_sem=w_r,
                    device_id={"dp": dp_x(k)}, device_id_type=MESH,
                ).start()
            pltpu.make_async_copy(weights[i].at[:, cols(x)], wq.at[i, x], w_l.at[i]).start()

    def y_copy(odd, way, j, hh, turn):
        to = right if way == 0 else left
        return pltpu.make_async_remote_copy(
            src_ref=xq.at[hh, odd, j], dst_ref=xq.at[hh, odd, j],
            send_sem=y_s.at[odd, way, turn, j], recv_sem=y_r.at[odd, way, turn, j],
            device_id={"dp": to * NX + x}, device_id_type=MESH,
        )

    def arrived(odd, way, turn, j):
        y_copy(odd, way, j, h, turn).wait_recv()

    def forward(odd, turn):
        arrived(odd, 0, 0, turn)
        y_copy(odd, 0, turn, left, 1).start()
        arrived(odd, 1, 0, 2 + turn)
        y_copy(odd, 1, 2 + turn, right, 1).start()

    def others_arrived(odd):
        for j in range(2):
            arrived(odd, 0, 0, 2 + j)
            arrived(odd, 1, 0, j)

    def far_arrived(odd):
        for j in range(2):
            arrived(odd, 0, 1, j)
            arrived(odd, 1, 1, 2 + j)

    def take(odd, j, own):
        if own:
            keep(0).wait()
            keep(1).wait()
        drain(recv.at[odd, pl.ds(j * n_exp, n_exp - 2 * own)], disp_r.at[odd, j])
        for kind in range(2):
            for g in range(rows // 16):
                xq[h, odd, j, kind, 16 * g:16 * (g + 1), :] = jnp.concatenate(
                    [recv[odd, j * n_exp + kind * (n_exp // 2) + 8 * g + i] for i in range(8)],
                    axis=0,
                )
        for way in range(2):
            y_copy(odd, way, j, h, 0).start()

    for turn in range(4):
        k = (0, 1, 3, 2)[turn]
        take(0, peer_x(k), k == 0)
        if turn == 1:
            drain_sent(0)
            dispatch(1)
    exchange_weights()
    forward(0, 0)
    for k in (0, 1, 3, 2):
        take(1, peer_x(k), False)
    forward(0, 1)

    def chunk(kind, o):
        return jnp.concatenate(
            [xq[hh, odd, j, kind] for hh, odd in chunks[o] for j in range(NX)], axis=0
        )

    def partial_sums(o):
        both = wq[0:2].reshape(2 * NX * ff, quarter)
        down = wq[2].reshape(NX * ff, quarter)
        pre = lax.dot_general(both, chunk(0, o), NT, preferred_element_type=F32)
        back = lax.dot_general(down, chunk(1, o), NT, preferred_element_type=F32)
        parts = (pre[: NX * ff], pre[NX * ff :], back)
        for i in range(3):
            piece = parts[i].reshape(NX, ff, -1)
            pown[o][:, i] = piece
            if psend[o].dtype != F32:
                psend[o][:, i] = piece.astype(BF16)
        source = pown[o] if o in WIDE else psend[o]
        for k in (2, 1, 3):
            pltpu.make_async_remote_copy(
                src_ref=source.at[peer_x(k)], dst_ref=precv[o].at[k - 1],
                send_sem=rs_s.at[o], recv_sem=rs_r.at[o],
                device_id={"dp": dp_x(k)}, device_id_type=MESH,
            ).start()

    def factors(o):
        drain(precv[o], rs_r.at[o])
        total = []
        for i in range(3):
            v = pown[o][x, i]
            for k in range(3):
                v = v + precv[o][k, i].astype(F32)
            total.append(v)
        gate_pre, up_pre, back_grad = total
        sig = jax.nn.sigmoid(gate_pre)
        act = gate_pre * sig
        fac[o][0, x] = (back_grad * up_pre * sig * (1.0 + gate_pre * (1.0 - sig))).astype(BF16)
        fac[o][1, x] = (back_grad * act).astype(BF16)
        fac[o][2, x] = (act * up_pre).astype(BF16)
        for k in (2, 1, 3):
            pltpu.make_async_remote_copy(
                src_ref=fac[o].at[:, x], dst_ref=fac[o].at[:, x],
                send_sem=ag_s.at[o], recv_sem=ag_r.at[o],
                device_id={"dp": dp_x(k)}, device_id_type=MESH,
            ).start()

    outs = (og, ou, od)
    last = len(chunks) - 1

    def products(o):
        drain(fac[o].at[:, pl.ds(0, 3)], ag_r.at[o])
        for i in range(3):
            f = fac[o][i].reshape(NX * ff, -1)
            term = jnp.dot(f, chunk(1 if i == 2 else 0, o), preferred_element_type=F32)
            if o == 0:
                acc[i] = term
            elif o < last:
                acc[i] += term
            else:
                gbuf[i] = (acc[i] + term).astype(BF16).reshape(NX, ff, quarter)
                for k in (2, 1, 3):
                    pltpu.make_async_remote_copy(
                        src_ref=gbuf.at[i, peer_x(k)], dst_ref=outs[i].at[:, cols(x)],
                        send_sem=o_s.at[i], recv_sem=o_r.at[i],
                        device_id={"dp": dp_x(k)}, device_id_type=MESH,
                    ).start()
                pltpu.make_async_copy(gbuf.at[i, x], outs[i].at[:, cols(x)], o_l.at[i]).start()

    drain(wq.at[:, pl.ds(0, 3)], w_r)
    for i in range(3):
        pltpu.make_async_copy(weights[i].at[:, cols(x)], wq.at[i, x], w_l.at[i]).wait()
    partial_sums(0)
    partial_sums(2)
    others_arrived(0)
    partial_sums(1)
    factors(0)
    factors(2)
    forward(1, 0)
    forward(1, 1)
    products(0)
    factors(1)
    others_arrived(1)
    partial_sums(3)
    products(2)
    far_arrived(0)
    partial_sums(4)
    products(1)
    factors(3)
    factors(4)
    products(3)
    far_arrived(1)
    partial_sums(5)
    products(4)
    factors(5)
    products(5)

    for odd in range(2):
        for way in range(2):
            for j in range(NX):
                y_copy(odd, way, j, h, 0).wait_send()
            for j in range(2):
                y_copy(odd, way, 2 * way + j, h, 1).wait_send()
    drain_sent(1)
    drain(wq.at[:, pl.ds(0, 3)], w_s)
    for o in range(len(chunks)):
        drain(precv[o], rs_s.at[o])
        drain(fac[o].at[:, pl.ds(0, 3)], ag_s.at[o])
    for i in range(3):
        drain(gbuf.at[i, pl.ds(0, 3)], o_r.at[i])
        drain(gbuf.at[i, pl.ds(0, 3)], o_s.at[i])
        pltpu.make_async_copy(gbuf.at[i, x], outs[i].at[:, cols(x)], o_l.at[i]).wait()


def local(tokens, expert_ids, gate_probs, out_grad, w_gate, w_up, w_down):
    n_exp = w_gate.shape[0] * lax.axis_size("expert")
    tok_rows = expert_ids.shape[0]
    d = tokens.shape[1]
    ff = w_gate.shape[1]
    quarter = d // NX
    slots = n_exp * CAP
    rows = slots // 2
    expert_range = jnp.arange(n_exp, dtype=jnp.int32)
    hit = expert_ids[None, :, :] == expert_range[:, None, None]
    member = jnp.sum(hit.astype(F32), axis=2)
    prob = jnp.sum(jnp.where(hit, gate_probs[None, :, :], 0.0), axis=2)
    t = jnp.arange(tok_rows, dtype=jnp.int32)
    earlier = (t[:, None] < t[None, :]).astype(BF16)
    rank = jnp.dot(member.astype(BF16), earlier, preferred_element_type=F32)
    slot = jnp.arange(CAP, dtype=jnp.int32).astype(F32)
    pick = member[:, None, :] * (rank[:, None, :] == slot[None, :, None]).astype(F32)
    slot_prob = jnp.sum(pick * prob[:, None, :], axis=2).reshape(slots)
    picker = pick.reshape(slots, tok_rows).astype(BF16)
    sent_x = jnp.dot(picker, tokens, preferred_element_type=F32).astype(BF16)
    sent_dy = (
        jnp.dot(picker, out_grad, preferred_element_type=F32) * slot_prob[:, None]
    ).astype(BF16)
    sent_x = sent_x.reshape(n_exp, CAP, d)
    sent_dy = sent_dy.reshape(n_exp, CAP, d)
    dma = pltpu.SemaphoreType.DMA
    grads = pl.pallas_call(
        kernel,
        out_shape=[jax.ShapeDtypeStruct((ff, d), BF16)] * 3,
        in_specs=[pl.BlockSpec(memory_space=pl.ANY)] * 5,
        out_specs=[pl.BlockSpec(memory_space=pl.ANY)] * 3,
        scratch_shapes=[
            pltpu.VMEM((2, NX * n_exp, CAP, quarter), BF16),
            pltpu.VMEM((NH, 2, NX, 2, rows, quarter), BF16),
            pltpu.VMEM((3, NX, ff, quarter), BF16),
            [pltpu.VMEM((NX, 3, ff, w * rows), F32) for w in WIDTHS],
            [
                pltpu.VMEM((1, 1, 8, 128), F32)
                if o in WIDE
                else pltpu.VMEM((NX, 3, ff, w * rows), BF16)
                for o, w in enumerate(WIDTHS)
            ],
            [
                pltpu.VMEM((3, 3, ff, w * rows), F32 if o in WIDE else BF16)
                for o, w in enumerate(WIDTHS)
            ],
            [pltpu.VMEM((3, NX, ff, w * rows), BF16) for w in WIDTHS],
            pltpu.VMEM((3, NX * ff, quarter), F32),
            pltpu.VMEM((3, NX, ff, quarter), BF16),
            dma((2,)), dma((2, NX)), dma((2,)),
            dma(()), dma(()), dma((3,)),
            dma((2, 2, 2, NX)), dma((2, 2, 2, NX)),
            dma((6,)), dma((6,)), dma((6,)), dma((6,)),
            dma((3,)), dma((3,)), dma((3,)),
        ],
        compiler_params=pltpu.CompilerParams(
            collective_id=0, has_side_effects=True, vmem_limit_bytes=56 * 1024 * 1024
        ),
    )(sent_x, sent_dy, w_gate[0], w_up[0], w_down[0])
    return tuple(g[None] for g in grads)


def solution(mesh):
    in_specs = (
        P(("expert", "dp"), None),
        P(("expert", "dp"), None),
        P(("expert", "dp"), None),
        P(("expert", "dp"), None),
        P("expert", "dp", None),
        P("expert", "dp", None),
        P("expert", "dp", None),
    )
    out_specs = (P("expert", "dp", None), P("expert", "dp", None), P("expert", "dp", None))
    return jax.shard_map(local, mesh=mesh, in_specs=in_specs, out_specs=out_specs, check_vma=False)
```

time: 154 us -> 136 us (0.88)
  the two profiles are of different devices: /device:TPU:10 before, /device:TPU:88 now
where the time goes in v2:
time: 136 us
  Pallas kernels  127 us (93%)
  local copies, waits for them, and re-layouts  6.62 us (5%)
    pallas_call x1, Pallas kernels, local(): pl.pallas_call(kernel, out_shape=[jax.ShapeDtypeStruct((ff, d), BF16)] *...  127 us
    unnamed x15, local copies, waits for them, and re-layouts  4.5 us

profile of v2, /device:TPU:88, one launch (start us, length us, event | category | flops | bytes accessed | tf_op | source)
XLA Modules:
  0.0 135.5 jit_solution(9899816524434642341)
XLA Ops:
  0.6 0.0 copy-start
  0.7 0.0 copy-start.4
  0.7 0.0 copy-start.5
  0.7 0.1 eq.43
  0.8 0.6 copy-done.4
  1.4 0.0 copy-done.5
  1.4 0.1 select_reduce_fusion
  1.5 0.1 fusion.1
  1.7 0.2 fusion.3
  1.9 0.1 mul.36
  2.0 0.1 select_convert_fusion
  2.1 0.0 copy-done
  2.1 0.0 copy-start.1
  2.1 0.3 fusion
  2.4 0.9 reshape.27.sdy
  3.3 0.0 copy-done.1
  3.3 0.3 convolution_convert_fusion
  3.6 0.9 reshape.26.sx
  4.5 127.1 %shard_map.94 = (bf16[64,3584]{1,0:T(8,128)(2,1)}, bf16[64,3584]{1,0:T(8,128)(2,1)}, bf16[64,3584]{1,0:T(8,128)(2,1)}) custom-call(bf16[32,2,3584]{2,1,0:T(2,128)(2,1)} %reshape.26.sx, bf16[32,2,3584]{2,1,0:T(2,128)(2,1)} %reshape.27.sdy, bf16[64,3584]{1,0:T(8,128)(2,1)} %bitcast.15, bf16[64,3584]{1,0:T(8,128)(2,1)} %bitcast.16, bf16[64,3584]{1,0:T(8,128)(2,1)} %bitcast.17), custom_call_target="tpu_custom_call" | custom-call | tf_op jit(solution)/shard_map/pallas_call | solution.py:317
  131.7 0.0 copy-start.3
  131.7 1.9 %copy.21 = bf16[1,64,3584]{2,1,0:T(8,128)(2,1)} copy(bf16[1,64,3584]{2,1,0:T(8,128)(2,1)} %bitcast.14) | data formatting | bytes 917504
  133.6 0.0 copy-done.3
  133.6 0.0 copy-start.2
  133.6 0.8 copy.22
  134.3 0.4 copy-done.2
  134.8 0.8 copy.23
  (4 shorter events, 0.0 us)
Async XLA Ops:
  0.6 1.5 %copy-start = (bf16[128,3584]{1,0:T(8,128)(2,1)S(1)}, bf16[128,3584]{1,0:T(8,128)(2,1)}, u32[]{:S(2)}) copy-start(bf16[128,3584]{1,0:T(8,128)(2,1)} %param.10) | copy-start | bytes 2752516
  0.7 0.8 copy-start.4
  0.7 0.8 copy-start.5
  2.1 1.2 copy-start.1
  131.7 1.9 %copy-start.3 = (bf16[64,3584]{1,0:T(8,128)(2,1)S(1)}, bf16[64,3584]{1,0:T(8,128)(2,1)}, u32[]{:S(2)}) copy-start(bf16[64,3584]{1,0:T(8,128)(2,1)} %get-tuple-element.7) | copy-start | bytes 1376260
  133.6 1.2 copy-start.2

commit v3 on v2

--- a/solution.py
+++ b/solution.py
@@ -19,9 +19,9 @@
 
 
 def kernel(
-    sx, sdy, wg, wu, wd, og, ou, od,
-    recv, xq, wq, pown, psend, precv, fac, acc, gbuf,
-    disp_s, disp_r, disp_l, w_s, w_r, w_l,
+    ids, probs, tokens, out_grad, wg, wu, wd, og, ou, od,
+    tok, sx, sdy, recv, xq, wq, pown, psend, precv, fac, acc, gbuf,
+    tok_l, disp_s, disp_r, disp_l, w_s, w_r, w_l,
     y_s, y_r, rs_s, rs_r, ag_s, ag_r, o_s, o_r, o_l,
 ):
     n_exp = sx.shape[0]
@@ -71,6 +71,12 @@
     def drain(ref, sem):
         pltpu.make_async_copy(ref, ref, sem).wait()
 
+    staged = (
+        pltpu.make_async_copy(tokens, tok.at[0], tok_l.at[0]),
+        pltpu.make_async_copy(out_grad, tok.at[1], tok_l.at[1]),
+    )
+    for copy in staged:
+        copy.start()
     barrier = pltpu.get_barrier_semaphore()
 
     for k in range(NX):
@@ -83,9 +89,35 @@
             experts(greet, odd, k > 0)
     for hh in (left, right):
         pl.semaphore_signal(barrier, inc=1, device_id={"dp": hh * NX + x}, device_id_type=MESH)
+    slots = n_exp * CAP
+    n_tok = tok.shape[1]
+    row = lax.broadcasted_iota(jnp.int32, (slots, n_tok), 0)
+    expert_of = row >> 1
+    slot_of = (row & 1).astype(F32)
+    member = jnp.zeros((slots, n_tok), F32)
+    prob = jnp.zeros((slots, n_tok), F32)
+    for k in range(ids.shape[0]):
+        hit = ids[k:k + 1, :] == expert_of
+        member = member + jnp.where(hit, 1.0, 0.0)
+        prob = prob + jnp.where(hit, probs[k:k + 1, :], 0.0)
+    before = lax.broadcasted_iota(jnp.int32, (n_tok, n_tok), 0)
+    after = lax.broadcasted_iota(jnp.int32, (n_tok, n_tok), 1)
+    earlier = jnp.where(before < after, 1.0, 0.0).astype(BF16)
+    rank = jnp.dot(member.astype(BF16), earlier, preferred_element_type=F32)
+    pick = jnp.where(rank == slot_of, member, 0.0)
+    slot_prob = jnp.sum(pick * prob, axis=1, keepdims=True)
+    picker = pick.astype(BF16)
+    sent = (sx, sdy)
+    for kind in range(2):
+        staged[kind].wait()
+        picked = jnp.dot(picker, tok[kind], preferred_element_type=F32)
+        if kind == 1:
+            picked = picked * slot_prob
+        picked = picked.astype(BF16)
+        for e in range(n_exp):
+            sent[kind][e] = picked[2 * e:2 * e + 2]
+
     pl.semaphore_wait(barrier, n_peer - 1 + 2)
-
-    sent = (sx, sdy)
 
     def slab(odd, kind):
         return recv.at[odd, (x * 2 + kind) * (n_exp // 2) + me // 2]
@@ -102,17 +134,20 @@
                 def send(e, k=k, kind=kind):
                     pltpu.make_async_remote_copy(
                         src_ref=sent[kind].at[e, :, cols(peer_x(k))], dst_ref=slab(odd, kind),
-                        send_sem=disp_s.at[odd], recv_sem=disp_r.at[odd, x],
+                        send_sem=disp_s.at[odd, k], recv_sem=disp_r.at[odd, x],
                         device_id={"expert": e, "dp": dp_x(k)}, device_id_type=MESH,
                     ).start()
 
                 experts(send, odd, k > 0)
 
-    def drain_sent(odd):
-        drain(recv.at[odd, pl.ds(0, n_peer - 2 + 2 * odd)], disp_s.at[odd])
+    def drain_sent(odd, k):
+        own = k == 0 and not odd
+        drain(recv.at[odd, pl.ds(0, n_exp - 2 * own)], disp_s.at[odd, k])
 
     weights = (wg, wu, wd)
     dispatch(0)
+    drain_sent(0, 0)
+    dispatch(1)
     def exchange_weights():
         for i in range(3):
             for k in (2, 1, 3):
@@ -167,9 +202,6 @@
     for turn in range(4):
         k = (0, 1, 3, 2)[turn]
         take(0, peer_x(k), k == 0)
-        if turn == 1:
-            drain_sent(0)
-            dispatch(1)
     exchange_weights()
     forward(0, 0)
     for k in (0, 1, 3, 2):
@@ -254,19 +286,19 @@
     factors(2)
     forward(1, 0)
     forward(1, 1)
-    products(0)
     factors(1)
     others_arrived(1)
     partial_sums(3)
+    products(0)
     products(2)
     far_arrived(0)
     partial_sums(4)
+    factors(3)
     products(1)
-    factors(3)
     factors(4)
-    products(3)
     far_arrived(1)
     partial_sums(5)
+    products(3)
     products(4)
     factors(5)
     products(5)
@@ -277,7 +309,10 @@
                 y_copy(odd, way, j, h, 0).wait_send()
             for j in range(2):
                 y_copy(odd, way, 2 * way + j, h, 1).wait_send()
-    drain_sent(1)
+    for k in range(NX):
+        if k > 0:
+            drain_sent(0, k)
+        drain_sent(1, k)
     drain(wq.at[:, pl.ds(0, 3)], w_s)
     for o in range(len(chunks)):
         drain(precv[o], rs_s.at[o])
@@ -288,38 +323,46 @@
         pltpu.make_async_copy(gbuf.at[i, x], outs[i].at[:, cols(x)], o_l.at[i]).wait()
 
 
+def hand_on(*refs):
+    sources, results, held, sem_in, sem_out = refs[:3], refs[3:6], refs[6], refs[7], refs[8]
+    half = held.shape[2]
+    coming, going = [], []
+    for i in range(3):
+        for part in range(2):
+            span = pl.ds(part * half, half)
+            coming.append(
+                pltpu.make_async_copy(sources[i].at[span], held.at[i, part], sem_in.at[i, part])
+            )
+            going.append(
+                pltpu.make_async_copy(held.at[i, part], results[i].at[span], sem_out.at[i, part])
+            )
+    for copy in coming:
+        copy.start()
+    for first, second in zip(coming, going):
+        first.wait()
+        second.start()
+    for copy in going:
+        copy.wait()
+
+
 def local(tokens, expert_ids, gate_probs, out_grad, w_gate, w_up, w_down):
     n_exp = w_gate.shape[0] * lax.axis_size("expert")
     tok_rows = expert_ids.shape[0]
     d = tokens.shape[1]
     ff = w_gate.shape[1]
     quarter = d // NX
-    slots = n_exp * CAP
-    rows = slots // 2
-    expert_range = jnp.arange(n_exp, dtype=jnp.int32)
-    hit = expert_ids[None, :, :] == expert_range[:, None, None]
-    member = jnp.sum(hit.astype(F32), axis=2)
-    prob = jnp.sum(jnp.where(hit, gate_probs[None, :, :], 0.0), axis=2)
-    t = jnp.arange(tok_rows, dtype=jnp.int32)
-    earlier = (t[:, None] < t[None, :]).astype(BF16)
-    rank = jnp.dot(member.astype(BF16), earlier, preferred_element_type=F32)
-    slot = jnp.arange(CAP, dtype=jnp.int32).astype(F32)
-    pick = member[:, None, :] * (rank[:, None, :] == slot[None, :, None]).astype(F32)
-    slot_prob = jnp.sum(pick * prob[:, None, :], axis=2).reshape(slots)
-    picker = pick.reshape(slots, tok_rows).astype(BF16)
-    sent_x = jnp.dot(picker, tokens, preferred_element_type=F32).astype(BF16)
-    sent_dy = (
-        jnp.dot(picker, out_grad, preferred_element_type=F32) * slot_prob[:, None]
-    ).astype(BF16)
-    sent_x = sent_x.reshape(n_exp, CAP, d)
-    sent_dy = sent_dy.reshape(n_exp, CAP, d)
+    rows = n_exp
     dma = pltpu.SemaphoreType.DMA
     grads = pl.pallas_call(
         kernel,
         out_shape=[jax.ShapeDtypeStruct((ff, d), BF16)] * 3,
-        in_specs=[pl.BlockSpec(memory_space=pl.ANY)] * 5,
+        in_specs=[pl.BlockSpec(memory_space=pltpu.VMEM)] * 2
+        + [pl.BlockSpec(memory_space=pl.ANY)] * 5,
         out_specs=[pl.BlockSpec(memory_space=pl.ANY)] * 3,
         scratch_shapes=[
+            pltpu.VMEM((2, tok_rows, d), BF16),
+            pltpu.VMEM((n_exp, CAP, d), BF16),
+            pltpu.VMEM((n_exp, CAP, d), BF16),
             pltpu.VMEM((2, NX * n_exp, CAP, quarter), BF16),
             pltpu.VMEM((NH, 2, NX, 2, rows, quarter), BF16),
             pltpu.VMEM((3, NX, ff, quarter), BF16),
@@ -337,7 +380,8 @@
             [pltpu.VMEM((3, NX, ff, w * rows), BF16) for w in WIDTHS],
             pltpu.VMEM((3, NX * ff, quarter), F32),
             pltpu.VMEM((3, NX, ff, quarter), BF16),
-            dma((2,)), dma((2, NX)), dma((2,)),
+            dma((2,)),
+            dma((2, NX)), dma((2, NX)), dma((2,)),
             dma(()), dma(()), dma((3,)),
             dma((2, 2, 2, NX)), dma((2, 2, 2, NX)),
             dma((6,)), dma((6,)), dma((6,)), dma((6,)),
@@ -346,7 +390,14 @@
         compiler_params=pltpu.CompilerParams(
             collective_id=0, has_side_effects=True, vmem_limit_bytes=56 * 1024 * 1024
         ),
-    )(sent_x, sent_dy, w_gate[0], w_up[0], w_down[0])
+    )(expert_ids.T, gate_probs.T, tokens, out_grad, w_gate[0], w_up[0], w_down[0])
+    grads = pl.pallas_call(
+        hand_on,
+        out_shape=[jax.ShapeDtypeStruct((ff, d), BF16)] * 3,
+        in_specs=[pl.BlockSpec(memory_space=pl.ANY)] * 3,
+        out_specs=[pl.BlockSpec(memory_space=pl.ANY)] * 3,
+        scratch_shapes=[pltpu.VMEM((3, 2, ff // 2, d), BF16), dma((3, 2)), dma((3, 2))],
+    )(*grads)
     return tuple(g[None] for g in grads)
 
 

time: 136 us -> 128 us (0.941)
  the two profiles are of different devices: /device:TPU:88 before, /device:TPU:8 now
where the time goes in v3:
time: 128 us
  Pallas kernels  127 us (99%)
    pallas_call x1, Pallas kernels, local(): pl.pallas_call(kernel, out_shape=[jax.ShapeDtypeStruct((ff, d), BF16)] *...  125 us

profile of v3, /device:TPU:8, one launch (start us, length us, event | category | flops | bytes accessed | tf_op | source)
XLA Modules:
  0.0 127.8 jit_solution(18223765034934867327)
XLA Ops:
  0.6 125.0 %shard_map.94 = (bf16[64,3584]{1,0:T(8,128)(2,1)}, bf16[64,3584]{1,0:T(8,128)(2,1)}, bf16[64,3584]{1,0:T(8,128)(2,1)}) custom-call(s32[8,128]{1,0:T(8,128)} %bitcast.11, f32[8,128]{1,0:T(8,128)} %bitcast.12, bf16[128,3584]{1,0:T(8,128)(2,1)} %tokens.1, bf16[128,3584]{1,0:T(8,128)(2,1)} %out_grad.1, bf16[64,3584]{1,0:T(8,128)(2,1)} %bitcast.8, ...), custom_call_target="tpu_custom_call" | custom-call | tf_op jit(solution)/shard_map/pallas_call | solution.py:356
  125.6 2.2 %shard_map.95 = (bf16[64,3584]{1,0:T(8,128)(2,1)}, bf16[64,3584]{1,0:T(8,128)(2,1)}, bf16[64,3584]{1,0:T(8,128)(2,1)}) custom-call(bf16[64,3584]{1,0:T(8,128)(2,1)} %get-tuple-element.9.refs_0_, bf16[64,3584]{1,0:T(8,128)(2,1)} %get-tuple-element.10.refs_1_, bf16[64,3584]{1,0:T(8,128)(2,1)} %get-tuple-element.11.refs_2_), custom_call_target="tpu_custom_call" | custom-call | tf_op jit(solution)/shard_map/pallas_call | solution.py:394

commit v4 on v3

--- a/solution.py
+++ b/solution.py
@@ -146,7 +146,6 @@
 
     weights = (wg, wu, wd)
     dispatch(0)
-    drain_sent(0, 0)
     dispatch(1)
     def exchange_weights():
         for i in range(3):
@@ -203,9 +202,9 @@
         k = (0, 1, 3, 2)[turn]
         take(0, peer_x(k), k == 0)
     exchange_weights()
-    forward(0, 0)
     for k in (0, 1, 3, 2):
         take(1, peer_x(k), False)
+    forward(0, 0)
     forward(0, 1)
 
     def chunk(kind, o):
@@ -310,8 +309,7 @@
             for j in range(2):
                 y_copy(odd, way, 2 * way + j, h, 1).wait_send()
     for k in range(NX):
-        if k > 0:
-            drain_sent(0, k)
+        drain_sent(0, k)
         drain_sent(1, k)
     drain(wq.at[:, pl.ds(0, 3)], w_s)
     for o in range(len(chunks)):

time: 128 us -> 124 us (0.969)
  the two profiles are of different devices: /device:TPU:8 before, /device:TPU:2 now
where the time goes in v4:
time: 124 us
  Pallas kernels  124 us (100%)
    pallas_call x1, Pallas kernels, local(): pl.pallas_call(kernel, out_shape=[jax.ShapeDtypeStruct((ff, d), BF16)] *...  121 us

profile of v4, /device:TPU:2, one launch (start us, length us, event | category | flops | bytes accessed | tf_op | source)
XLA Modules:
  0.0 124.2 jit_solution(1581869199424448848)
XLA Ops:
  0.6 121.3 %shard_map.94 = (bf16[64,3584]{1,0:T(8,128)(2,1)}, bf16[64,3584]{1,0:T(8,128)(2,1)}, bf16[64,3584]{1,0:T(8,128)(2,1)}) custom-call(s32[8,128]{1,0:T(8,128)} %bitcast.11, f32[8,128]{1,0:T(8,128)} %bitcast.12, bf16[128,3584]{1,0:T(8,128)(2,1)} %tokens.1, bf16[128,3584]{1,0:T(8,128)(2,1)} %out_grad.1, bf16[64,3584]{1,0:T(8,128)(2,1)} %bitcast.8, ...), custom_call_target="tpu_custom_call" | custom-call | tf_op jit(solution)/shard_map/pallas_call | solution.py:354
  121.9 2.2 %shard_map.95 = (bf16[64,3584]{1,0:T(8,128)(2,1)}, bf16[64,3584]{1,0:T(8,128)(2,1)}, bf16[64,3584]{1,0:T(8,128)(2,1)}) custom-call(bf16[64,3584]{1,0:T(8,128)(2,1)} %get-tuple-element.9.refs_0_, bf16[64,3584]{1,0:T(8,128)(2,1)} %get-tuple-element.10.refs_1_, bf16[64,3584]{1,0:T(8,128)(2,1)} %get-tuple-element.11.refs_2_), custom_call_target="tpu_custom_call" | custom-call | tf_op jit(solution)/shard_map/pallas_call | solution.py:392

commit v5 on v4

--- a/solution.py
+++ b/solution.py
@@ -297,9 +297,9 @@
     factors(4)
     far_arrived(1)
     partial_sums(5)
+    factors(5)
     products(3)
     products(4)
-    factors(5)
     products(5)
 
     for odd in range(2):

time: 124 us -> 124 us (level)
  no operation moved by 1% of the time
where the time goes in v5:
time: 124 us
  Pallas kernels  124 us (100%)
    pallas_call x1, Pallas kernels, local(): pl.pallas_call(kernel, out_shape=[jax.ShapeDtypeStruct((ff, d), BF16)] *...  121 us

profile of v5, /device:TPU:2, one launch (start us, length us, event | category | flops | bytes accessed | tf_op | source)
XLA Modules:
  0.0 124.2 jit_solution(5535606326067886611)
XLA Ops:
  0.6 121.3 %shard_map.94 = (bf16[64,3584]{1,0:T(8,128)(2,1)}, bf16[64,3584]{1,0:T(8,128)(2,1)}, bf16[64,3584]{1,0:T(8,128)(2,1)}) custom-call(s32[8,128]{1,0:T(8,128)} %bitcast.11, f32[8,128]{1,0:T(8,128)} %bitcast.12, bf16[128,3584]{1,0:T(8,128)(2,1)} %tokens.1, bf16[128,3584]{1,0:T(8,128)(2,1)} %out_grad.1, bf16[64,3584]{1,0:T(8,128)(2,1)} %bitcast.8, ...), custom_call_target="tpu_custom_call" | custom-call | tf_op jit(solution)/shard_map/pallas_call | solution.py:354
  121.9 2.2 %shard_map.95 = (bf16[64,3584]{1,0:T(8,128)(2,1)}, bf16[64,3584]{1,0:T(8,128)(2,1)}, bf16[64,3584]{1,0:T(8,128)(2,1)}) custom-call(bf16[64,3584]{1,0:T(8,128)(2,1)} %get-tuple-element.9.refs_0_, bf16[64,3584]{1,0:T(8,128)(2,1)} %get-tuple-element.10.refs_1_, bf16[64,3584]{1,0:T(8,128)(2,1)} %get-tuple-element.11.refs_2_), custom_call_target="tpu_custom_call" | custom-call | tf_op jit(solution)/shard_map/pallas_call | solution.py:392
